TPU v7x, 32 devices: a whole 2x2x4 slice. The times are simulated.
32 devices in a mesh: inp: 4 (over y, core), hid: 8 (over z, x).
Axes of the slice: x: 2, y: 2, z: 4, core: 2. Of those that a mesh axis runs over, the one named last changes fastest.
Arguments:
- inputs: bfloat16 [128, 16384], P(None, 'inp'), may hold values from -6 to 6
- out_grad: bfloat16 [128, 16384], P(None, 'inp'), may hold values from -6 to 6
- gate_index: int32 [8192, 26624], P('inp', 'hid'), may hold values from 0 to 255, as said below
- up_index: int32 [8192, 26624], P('inp', 'hid'), may hold values from 0 to 255, as said below
- down_index: int32 [13312, 16384], P('hid', 'inp'), may hold values from 0 to 255, as said below
- gate_table: float32 [16, 26624], P(None, 'hid'), may hold values from -0.046875 to 0.046875
- up_table: float32 [16, 26624], P(None, 'hid'), may hold values from -0.046875 to 0.046875
- down_table: float32 [16, 16384], P(None, 'inp'), may hold values from -0.0390625 to 0.0390625
Outputs:
- input_grad: bfloat16 [128, 16384], P('hid', 'inp')
- gate_table_grad: float32 [16, 26624], P(None, 'hid')
- up_table_grad: float32 [16, 26624], P(None, 'hid')
- down_table_grad: float32 [16, 16384], P(None, 'inp')
Inputs may be any that keep to these rules, and one draw needn't show every extreme that they name: `gate_index`: each word holds two independent 4-bit table entries. `up_index`: each word holds two independent 4-bit table entries. `down_index`: each word holds two independent 4-bit table entries.
All inputs are finite; a program needn't handle non-finite values.
Results may differ from a plain program's by a relative error of at most 0.0072.
Values may be sent and summed in bfloat16 or wider, within the bound.
A program may use at most 512 MiB of HBM per device.

v0:
```python
import math

import jax
import jax.numpy as jnp
from jax import lax
from jax.sharding import PartitionSpec as P


def unpack(packed):
    parts = [jnp.bitwise_and(jnp.right_shift(packed, 4 * nibble), 15) for nibble in range(2)]
    stacked = jnp.stack(parts, axis=1)
    return stacked.reshape(packed.shape[0] * 2, packed.shape[1])


def row_block(rows):
    return math.gcd(rows, 128)


def decode(indices, lookup):
    rows, cols = indices.shape
    block = row_block(rows)
    buckets = jnp.arange(16, dtype=jnp.int32)

    def decode_block(piece):
        chosen = jnp.where(piece[None, :, :] == buckets[:, None, None], lookup[:, None, :], 0.0)
        return jnp.sum(chosen, axis=0).astype(jnp.bfloat16)

    pieces = lax.map(decode_block, indices.reshape(rows // block, block, cols))
    return pieces.reshape(rows, cols)


def binned_product(left, right, indices):
    tokens, rows = left.shape
    cols = right.shape[1]
    block = row_block(rows)
    buckets = jnp.arange(16, dtype=jnp.int32)
    left_blocks = jnp.transpose(left.reshape(tokens, rows // block, block), (1, 0, 2))

    def bin_block(pair):
        left_piece, index_piece = pair
        grads = lax.dot_general(
            left_piece, right, (((0,), (0,)), ((), ())), preferred_element_type=jnp.float32
        )
        chosen = jnp.where(
            index_piece[None, :, :] == buckets[:, None, None], grads[None, :, :], 0.0
        )
        return jnp.sum(chosen, axis=1)

    partial_bins = lax.map(bin_block, (left_blocks, indices.reshape(rows // block, block, cols)))
    return jnp.sum(partial_bins, axis=0)


def contract_cols(left, right):
    return lax.dot_general(
        left, right, (((1,), (1,)), ((), ())), preferred_element_type=jnp.float32
    )


def local_hidden(pre_gate, pre_up, hidden_grad):
    sig_gate = jax.nn.sigmoid(pre_gate)
    silu_gate = pre_gate * sig_gate
    activ = (silu_gate * pre_up).astype(jnp.bfloat16)
    gate_grad = (hidden_grad * pre_up * sig_gate * (1.0 + pre_gate * (1.0 - sig_gate))).astype(
        jnp.bfloat16
    )
    up_grad = (hidden_grad * silu_gate).astype(jnp.bfloat16)
    return (activ, gate_grad, up_grad)


def shards(inputs, out_grad, gate_index, up_index, down_index, gate_table, up_table, down_table):
    tokens = inputs.shape[0]
    hidden_width = gate_index.shape[1]
    idx_gate = unpack(gate_index)
    idx_up = unpack(up_index)
    idx_down = unpack(down_index)
    w_gate = decode(idx_gate, gate_table)
    w_up = decode(idx_up, up_table)
    w_down = decode(idx_down, down_table)
    share = lax.psum_scatter(
        jnp.concatenate(
            [
                jnp.dot(inputs, w_gate, preferred_element_type=jnp.float32),
                jnp.dot(inputs, w_up, preferred_element_type=jnp.float32),
                contract_cols(out_grad, w_down),
            ],
            axis=1,
        ),
        "inp",
        scatter_dimension=0,
        tiled=True,
    )
    part_act, part_gate, part_up = local_hidden(
        share[:, :hidden_width],
        share[:, hidden_width : 2 * hidden_width],
        share[:, 2 * hidden_width :],
    )
    activ, gate_grad, up_grad = (
        lax.all_gather(part_act, "inp", axis=0, tiled=True),
        lax.all_gather(part_gate, "inp", axis=0, tiled=True),
        lax.all_gather(part_up, "inp", axis=0, tiled=True),
    )
    input_grad = lax.psum_scatter(
        contract_cols(gate_grad, w_gate) + contract_cols(up_grad, w_up),
        "hid",
        scatter_dimension=0,
        tiled=True,
    ).astype(jnp.bfloat16)
    gate_bins = binned_product(inputs, gate_grad, idx_gate)
    up_bins = binned_product(inputs, up_grad, idx_up)
    gate_sum, up_sum = lax.psum((gate_bins, up_bins), "inp")
    down_sum = lax.psum(binned_product(activ, out_grad, idx_down), "hid")
    scale = 1.0 / tokens
    return (input_grad, gate_sum * scale, up_sum * scale, down_sum * scale)


def solution(mesh):
    in_specs = (
        P(None, "inp"),
        P(None, "inp"),
        P("inp", "hid"),
        P("inp", "hid"),
        P("hid", "inp"),
        P(None, "hid"),
        P(None, "hid"),
        P(None, "inp"),
    )
    out_specs = (P("hid", "inp"), P(None, "hid"), P(None, "hid"), P(None, "inp"))
    return jax.shard_map(shards, mesh=mesh, in_specs=in_specs, out_specs=out_specs, check_vma=False)
```

profile of v0, /device:TPU:0, one launch (start us, length us, event | category | flops | bytes accessed | tf_op | source)
XLA Modules:
  0.0 2108.5 jit_solution(12354736842710685854)
XLA Ops:
  7.2 28.4 %and_bitcast_fusion.1 = (s32[1664,1,4096]{2,0,1:T(8,128)}, s32[1664,1,4096]{2,0,1:T(8,128)}) fusion(s32[1664,4096]{1,0:T(8,128)} %param.24), kind=kLoop, calls=%fused_computation.46 | loop fusion | flops 27262976 | bytes 81788928 | tf_op jit(solution)/shard_map/stack | solution.py:11
  35.6 36.3 %pad_add_fusion.2 = s32[1664,2,4096]{2,0,1:T(8,128)} fusion(s32[1664,1,4096]{2,0,1:T(8,128)} %get-tuple-element.389, s32[1664,1,4096]{2,0,1:T(8,128)} %get-tuple-element.388), kind=kLoop, calls=%fused_computation.44 | loop fusion | flops 13631488 | bytes 109051904 | tf_op jit(solution)/shard_map/stack | solution.py:11
  71.9 88.1 %copy.61 = s32[1664,2,4096]{2,1,0:T(2,128)} copy(s32[1664,2,4096]{2,0,1:T(8,128)} %pad_add_fusion.2) | data formatting | bytes 109051904 | tf_op jit(solution)/shard_map/stack | solution.py:11
  160.0 63.9 %reshape_reshape.14 = s32[26,128,4096]{2,1,0:T(8,128)} reshape(s32[1664,2,4096]{2,1,0:T(2,128)} %copy.61) | data formatting | bytes 109051904 | tf_op jit(solution)/shard_map/reshape;reshape | solution.py:28
  223.9 159.1 %while.68 = (s32[]{:T(128)}, bf16[26,128,4096]{2,1,0:T(8,128)(2,1)}, s32[26,128,4096]{2,1,0:T(8,128)}, f32[16,4096]{1,0:T(8,128)S(1)}, s32[]{:T(128)}) while((s32[]{:T(128)}, bf16[26,128,4096]{2,1,0:T(8,128)(2,1)}, s32[26,128,4096]{2,1,0:T(8,128)}, f32[16,4096]{1,0:T(8,128)S(1)}, s32[]{:T(128)}) %tuple.157), condition=%wide.region_8.9_spmd.clone, body=%wide.region_6.8_spmd.clone.sunk | while | flops 24641536 | bytes 9699405 | solution.py:28
  383.0 27.2 %and_bitcast_fusion.3 = (s32[2048,1,3328]{2,0,1:T(8,128)}, s32[2048,1,3328]{2,0,1:T(8,128)}) fusion(s32[2048,3328]{1,0:T(8,128)} %param.23), kind=kLoop, calls=%fused_computation.48 | loop fusion | flops 27262976 | bytes 81788928 | tf_op jit(solution)/shard_map/stack | solution.py:11
  410.1 36.6 %pad_add_fusion.1 = s32[2048,2,3328]{2,0,1:T(8,128)} fusion(s32[2048,1,3328]{2,0,1:T(8,128)} %get-tuple-element.387, s32[2048,1,3328]{2,0,1:T(8,128)} %get-tuple-element.386), kind=kLoop, calls=%fused_computation.43 | loop fusion | flops 13631488 | bytes 109051904 | tf_op jit(solution)/shard_map/stack | solution.py:11
  446.8 88.3 %copy.60 = s32[2048,2,3328]{2,1,0:T(2,128)} copy(s32[2048,2,3328]{2,0,1:T(8,128)} %pad_add_fusion.1) | data formatting | bytes 109051904 | tf_op jit(solution)/shard_map/stack | solution.py:11
  535.1 64.0 %reshape_reshape.13 = s32[32,128,3328]{2,1,0:T(8,128)} reshape(s32[2048,2,3328]{2,1,0:T(2,128)} %copy.60) | data formatting | bytes 109051904 | tf_op jit(solution)/shard_map/reshape;reshape | solution.py:28
  599.1 9.5 broadcast.36.clone
  608.6 167.2 %while.67 = (s32[]{:T(128)}, bf16[32,128,3328]{2,1,0:T(8,128)(2,1)}, s32[32,128,3328]{2,1,0:T(8,128)}, f32[16,3328]{1,0:T(8,128)S(1)}, s32[]{:T(128)}) while((s32[]{:T(128)}, bf16[32,128,3328]{2,1,0:T(8,128)(2,1)}, s32[32,128,3328]{2,1,0:T(8,128)}, f32[16,3328]{1,0:T(8,128)S(1)}, s32[]{:T(128)}) %tuple.158), condition=%wide.region_5.6_spmd.clone, body=%wide.region_3.5_spmd.clone.sunk | while | flops 20021248 | bytes 7880781 | solution.py:28
  775.8 27.2 %and_bitcast_fusion.5 = (s32[2048,1,3328]{2,0,1:T(8,128)}, s32[2048,1,3328]{2,0,1:T(8,128)}) fusion(s32[2048,3328]{1,0:T(8,128)} %param.22), kind=kLoop, calls=%fused_computation.50 | loop fusion | flops 27262976 | bytes 81788928 | tf_op jit(solution)/shard_map/stack | solution.py:11
  802.9 36.6 %pad_add_fusion = s32[2048,2,3328]{2,0,1:T(8,128)} fusion(s32[2048,1,3328]{2,0,1:T(8,128)} %get-tuple-element.385, s32[2048,1,3328]{2,0,1:T(8,128)} %get-tuple-element.384), kind=kLoop, calls=%fused_computation.42 | loop fusion | flops 13631488 | bytes 109051904 | tf_op jit(solution)/shard_map/stack | solution.py:11
  839.6 88.4 %copy.59 = s32[2048,2,3328]{2,1,0:T(2,128)} copy(s32[2048,2,3328]{2,0,1:T(8,128)} %pad_add_fusion) | data formatting | bytes 109051904 | tf_op jit(solution)/shard_map/stack | solution.py:11
  927.9 64.0 %reshape_reshape.12 = s32[32,128,3328]{2,1,0:T(8,128)} reshape(s32[2048,2,3328]{2,1,0:T(2,128)} %copy.59) | data formatting | bytes 109051904 | tf_op jit(solution)/shard_map/reshape;reshape | solution.py:28
  991.9 9.3 broadcast.36.clone.1
  1001.2 166.9 %while.66 = (s32[]{:T(128)}, bf16[32,128,3328]{2,1,0:T(8,128)(2,1)}, s32[32,128,3328]{2,1,0:T(8,128)}, f32[16,3328]{1,0:T(8,128)S(1)}, s32[]{:T(128)}) while((s32[]{:T(128)}, bf16[32,128,3328]{2,1,0:T(8,128)(2,1)}, s32[32,128,3328]{2,1,0:T(8,128)}, f32[16,3328]{1,0:T(8,128)S(1)}, s32[]{:T(128)}) %tuple.159), condition=%wide.region_2.3_spmd.clone, body=%wide.region_0.2_spmd.clone.sunk | while | flops 20021248 | bytes 7880781 | solution.py:28
  1168.1 12.8 convolution_bitcast_fusion.1
  1180.9 12.8 convolution_bitcast_fusion.2
  1193.7 12.6 convolution_bitcast_fusion
  1206.3 6.4 pad_maximum_fusion
  1221.6 50.3 %reduce-scatter.7.cloned.1.call-done = f32[32,9984]{1,0:T(8,128)} async-done(((f32[128,9984]{1,0:T(8,128)}), f32[32,9984]{1,0:T(8,128)}) %reduce-scatter.7.cloned.1.call-update) | async-done | bytes 1277968 | tf_op jit(solution)/shard_map/reduce_scatter | solution.py:79
  1273.5 8.4 all_gather.9
  1281.9 9.0 all_gather.10
  1294.5 205.9 %while.69 = (s32[]{:T(128)}, f32[32,16,3328]{2,1,0:T(8,128)}, s32[32,128,3328]{2,1,0:T(8,128)}, bf16[32,128,128]{2,1,0:T(8,128)(2,1)}, bf16[128,3328]{1,0:T(8,128)(2,1)S(1)}, /*index=5*/s32[]{:T(128)}) while((s32[]{:T(128)}, f32[32,16,3328]{2,1,0:T(8,128)}, s32[32,128,3328]{2,1,0:T(8,128)}, bf16[32,128,128]{2,1,0:T(8,128)(2,1)}, ...), condition=%wide.region_13.14_spmd.clone, body=%wide.region_11.13_spmd.clone.sunk | while | flops 129445888 | bytes 10043481 | solution.py:49
  1504.0 205.8 %while.70 = (s32[]{:T(128)}, f32[32,16,3328]{2,1,0:T(8,128)}, s32[32,128,3328]{2,1,0:T(8,128)}, bf16[32,128,128]{2,1,0:T(8,128)(2,1)}, bf16[128,3328]{1,0:T(8,128)(2,1)S(1)}, /*index=5*/s32[]{:T(128)}) while((s32[]{:T(128)}, f32[32,16,3328]{2,1,0:T(8,128)}, s32[32,128,3328]{2,1,0:T(8,128)}, bf16[32,128,128]{2,1,0:T(8,128)(2,1)}, ...), condition=%wide.region_18.19_spmd.clone, body=%wide.region_16.18_spmd.clone.sunk | while | flops 129445888 | bytes 10043481 | solution.py:49
  1709.8 9.5 all_gather.11
  1721.7 190.4 %while.71 = (s32[]{:T(128)}, f32[26,16,4096]{2,1,0:T(8,128)}, s32[26,128,4096]{2,1,0:T(8,128)}, bf16[26,128,128]{1,2,0:T(8,128)(2,1)}, bf16[128,4096]{1,0:T(8,128)(2,1)S(1)}, /*index=5*/s32[]{:T(128)}) while((s32[]{:T(128)}, f32[26,16,4096]{2,1,0:T(8,128)}, s32[26,128,4096]{2,1,0:T(8,128)}, bf16[26,128,128]{1,2,0:T(8,128)(2,1)}, ...), condition=%wide.region_23.24_spmd.clone, body=%wide.region_21.23_spmd.clone.sunk | while | flops 159318016 | bytes 12353625 | solution.py:49
  1920.1 15.5 fusion.25
  1939.6 16.1 convolution_add_fusion
  1957.6 71.1 %all-reduce.4.cloned.1.call-done = f32[16,4096]{1,0:T(8,128)} async-done(((f32[16,4096]{1,0:T(8,128)}), f32[16,4096]{1,0:T(8,128)}) %all-reduce.4.cloned.1.call-update) | async-done | bytes 262160 | tf_op jit(solution)/shard_map/psum | solution.py:111
  2030.4 69.8 %reduce-scatter.5.cloned.1.call-done = f32[16,4096]{1,0:T(8,128)} async-done(((f32[128,4096]{1,0:T(8,128)}), f32[16,4096]{1,0:T(8,128)}) %reduce-scatter.5.cloned.1.call-update) | async-done | bytes 262160 | tf_op jit(solution)/shard_map/reduce_scatter | solution.py:102
  (664 shorter events, 1130.3 us)
Async XLA Ops:
  7.2 1264.8 %reduce-scatter.7.cloned.1.call-start = ((), (), s32[]{:S(2)}) async-start(), calls=%async_computation.4 | async-start | bytes 6389760 | tf_op jit(solution)/shard_map/reduce_scatter | solution.py:79
  160.0 63.9 %copy-start.1 = (f32[16,4096]{1,0:T(8,128)S(1)}, f32[16,4096]{1,0:T(8,128)}, u32[]{:S(2)}) copy-start(f32[16,4096]{1,0:T(8,128)} %param.27) | copy-start | bytes 786436
  599.1 9.5 copy-start.2
  991.9 9.4 copy-start.3
  991.9 176.2 %copy-start.4 = (bf16[128,4096]{1,0:T(8,128)(2,1)S(1)}, bf16[128,4096]{1,0:T(8,128)(2,1)}, u32[]{:S(2)}) copy-start(bf16[128,4096]{1,0:T(8,128)(2,1)} %param.20) | copy-start | bytes 3145732
  1180.9 12.8 copy-start
  1218.6 737.2 %all-reduce.6.cloned.1.call-start = ((), (), s32[]{:S(2)}) async-start(), calls=%async_computation.5 | async-start | bytes 851968 | tf_op jit(solution)/shard_map/psum | solution.py:110
  1920.0 108.7 %all-reduce.4.cloned.1.call-start = ((), (), s32[]{:S(2)}) async-start(), calls=%async_computation.3 | async-start | bytes 524288 | tf_op jit(solution)/shard_map/psum | solution.py:111
  1939.6 160.6 %reduce-scatter.5.cloned.1.call-start = ((), (), s32[]{:S(2)}) async-start(), calls=%async_computation.2 | async-start | bytes 2359296 | tf_op jit(solution)/shard_map/reduce_scatter | solution.py:102
Sparse Core Ops, SparseCore 0:
  1218.7 53.1 reduce-scatter.6
  1920.1 33.5 all-reduce.5
  1957.6 71.0 all-reduce.3
  2032.1 68.0 reduce-scatter.4
where the time goes:
time: 2130 us; the launch traced here: 2110 us
  local copies, waits for them, and re-layouts  941 us (44%)
  other arithmetic  758 us (36%)
  waiting for transfers between devices  191 us (9%)
  matrix products  176 us (8%)
  blocking collectives  26.9 us (1%)
    reduce_sum x90, other arithmetic, bin_block(): return jnp.sum(chosen, axis=1)  285 us
    another operation x3, local copies, waits for them, and re-layouts, unpack(): stacked = jnp.stack(parts, axis=1)  265 us
    reduce_sum x90, other arithmetic, decode_block(): return jnp.sum(chosen, axis=0).astype(jnp.bfloat16)  256 us
    another operation x6, other arithmetic, unpack(): stacked = jnp.stack(parts, axis=1)  192 us
    another operation x3, local copies, waits for them, and re-layouts, decode(): pieces = lax.map(decode_block, indices.reshape(rows // block, block, cols))  192 us
    eq x90, local copies, waits for them, and re-layouts, bin_block(): index_piece[None, :, :] == buckets[:, None, None]  146 us
    eq x90, local copies, waits for them, and re-layouts, decode_block(): piece[None, :, :] == buckets[:, None, None]  145 us
    dot_general x90, matrix products, bin_block(): lax.dot_general(left_piece, right, (((0,), (0,)), ((), ())), preferred_el...  106 us
  transfers between devices with their start and end apart: 4, of which 3 were waited for; matrix products, arithmetic and copies ran while one was open for 2% of the time, Pallas kernels for 0%

commit v1 on v0

v1 whole, which is shorter than its diff:
```python
import functools
import math

import jax
import jax.numpy as jnp
from jax import lax
from jax.experimental import pallas as pl
from jax.experimental.pallas import tpu as pltpu
from jax.sharding import PartitionSpec as P

LANES = 128
SUB = 16
F32 = jnp.float32
BF16 = jnp.bfloat16


def divisor(size, most, unit=LANES):
    best = unit
    for cand in range(unit, most + 1, unit):
        if size % cand == 0:
            best = cand
    return best


def bit_masks(words, parity):
    return [(words & jnp.int16(1 << (4 * parity + bit))) != 0 for bit in range(4)]


def look_up(levels, masks):
    for mask in masks:
        levels = [jnp.where(mask, levels[i + 1], levels[i]) for i in range(0, len(levels), 2)]
    return levels[0]


def table_rows(table_ref, lanes):
    return [
        jnp.broadcast_to(table_ref[k : k + 1, lanes], (SUB, LANES)).astype(BF16)
        for k in range(16)
    ]


def decode_block(idx_ref, table, lanes, start, count, even_ref, odd_ref, base):
    for step in range(count // SUB):
        row = start + step * SUB
        words = idx_ref[pl.ds(row, SUB), lanes].astype(jnp.int16)
        dst = pl.ds(base + step * SUB, SUB)
        even_ref[dst, lanes] = look_up(table, bit_masks(words, 0))
        odd_ref[dst, lanes] = look_up(table, bit_masks(words, 1))


def up_kernel(block, xe_ref, xo_ref, gi_ref, ui_ref, gt_ref, ut_ref, pg_ref, pu_ref, ge_ref, go_ref, ue_ref, uo_ref):
    words, cols = gi_ref.shape
    for idx_ref, table_ref, even_ref, odd_ref, out_ref in (
        (gi_ref, gt_ref, ge_ref, go_ref, pg_ref),
        (ui_ref, ut_ref, ue_ref, uo_ref, pu_ref),
    ):
        for chunk in range(cols // LANES):
            lanes = slice(chunk * LANES, (chunk + 1) * LANES)
            table = table_rows(table_ref, lanes)

            def body(i, carry):
                start = pl.multiple_of(i * block, block)
                decode_block(idx_ref, table, lanes, start, block, even_ref, odd_ref, start)
                return carry

            lax.fori_loop(0, words // block, body, 0)
        out_ref[...] = jnp.dot(xe_ref[...], even_ref[...], preferred_element_type=F32) + jnp.dot(
            xo_ref[...], odd_ref[...], preferred_element_type=F32
        )


def up_products(x_even, x_odd, gate_index, up_index, gate_table, up_table):
    tokens = x_even.shape[0]
    words, width = gate_index.shape
    cols = divisor(width, 256)
    block = math.gcd(words, 128)
    whole = pl.BlockSpec((tokens, words), lambda j: (0, 0))
    tile = pl.BlockSpec((words, cols), lambda j: (0, j))
    lut = pl.BlockSpec((16, cols), lambda j: (0, j))
    pre = pl.BlockSpec((tokens, cols), lambda j: (0, j))
    weight = jax.ShapeDtypeStruct((words, width), BF16)
    return pl.pallas_call(
        functools.partial(up_kernel, block),
        grid=(width // cols,),
        in_specs=[whole, whole, tile, tile, lut, lut],
        out_specs=[pre, pre, tile, tile, tile, tile],
        out_shape=[jax.ShapeDtypeStruct((tokens, width), F32)] * 2 + [weight] * 4,
        name="up_products",
    )(x_even, x_odd, gate_index, up_index, gate_table, up_table)


def contract_cols(left, right):
    return lax.dot_general(left, right, (((1,), (1,)), ((), ())), preferred_element_type=F32)


def down_kernel(block, og_ref, di_ref, dt_ref, he_ref, ho_ref, even_ref, odd_ref):
    words, cols = di_ref.shape

    @pl.when(pl.program_id(0) == 0)
    def _():
        he_ref[...] = jnp.zeros_like(he_ref)
        ho_ref[...] = jnp.zeros_like(ho_ref)

    for chunk in range(cols // LANES):
        lanes = slice(chunk * LANES, (chunk + 1) * LANES)
        table = table_rows(dt_ref, lanes)

        def body(i, carry):
            start = pl.multiple_of(i * block, block)
            decode_block(di_ref, table, lanes, start, block, even_ref, odd_ref, start)
            return carry

        lax.fori_loop(0, words // block, body, 0)
    he_ref[...] += contract_cols(og_ref[...], even_ref[...])
    ho_ref[...] += contract_cols(og_ref[...], odd_ref[...])


def down_products(out_grad, down_index, down_table):
    tokens = out_grad.shape[0]
    words, width = down_index.shape
    cols = divisor(width, 256)
    block = math.gcd(words, 128)
    whole = pl.BlockSpec((tokens, words), lambda j: (0, 0))
    return pl.pallas_call(
        functools.partial(down_kernel, block),
        grid=(width // cols,),
        in_specs=[
            pl.BlockSpec((tokens, cols), lambda j: (0, j)),
            pl.BlockSpec((words, cols), lambda j: (0, j)),
            pl.BlockSpec((16, cols), lambda j: (0, j)),
        ],
        out_specs=[whole, whole],
        out_shape=[jax.ShapeDtypeStruct((tokens, words), F32)] * 2,
        scratch_shapes=[pltpu.VMEM((words, cols), BF16)] * 2,
        name="down_products",
    )(out_grad, down_index, down_table)


def leaves(value, masks):
    b0, b1, b2, b3 = masks
    zero = jnp.zeros_like(value)
    out = []
    for part in (jnp.where(b3, zero, value), jnp.where(b3, value, zero)):
        for piece in (jnp.where(b2, zero, part), jnp.where(b2, part, zero)):
            one = jnp.where(b1, piece, zero)
            out += [piece, jnp.where(b0, piece, zero), one, jnp.where(b0, one, zero)]
    return out


def bin_block(idx_ref, lanes, start, count, even_ref, odd_ref, acc_ref):
    sums = None
    for step in range(count // SUB):
        words = idx_ref[pl.ds(start + step * SUB, SUB), lanes].astype(jnp.int16)
        for parity, ref in ((0, even_ref), (1, odd_ref)):
            value = ref[step * SUB : (step + 1) * SUB, lanes].astype(BF16)
            parts = leaves(value, bit_masks(words, parity))
            sums = parts if sums is None else [a + b for a, b in zip(sums, parts)]
    for k, total in enumerate(sums):
        wide = total.astype(F32)
        acc_ref[8 * k : 8 * k + 8, lanes] += wide[:8] + wide[8:]


def write_bins(acc_ref, out_ref, scale):
    rows = [jnp.sum(acc_ref[8 * k : 8 * k + 8, :], axis=0, keepdims=True) for k in range(16)]
    for k in range(0, 16, 4):
        none, low, high, both = rows[k : k + 4]
        out_ref[k : k + 1, :] = ((none - low) - (high - both)) * scale
        out_ref[k + 1 : k + 2, :] = (low - both) * scale
        out_ref[k + 2 : k + 3, :] = (high - both) * scale
        out_ref[k + 3 : k + 4, :] = both * scale


def bin_columns(block, scale, left_even, left_odd, right, idx_ref, out_ref, acc_ref, pe_ref, po_ref):
    words, cols = idx_ref.shape
    acc_ref[...] = jnp.zeros_like(acc_ref)

    def body(i, carry):
        start = pl.multiple_of(i * block, block)
        pe_ref[...] = jnp.dot(left_even[pl.ds(start, block), :], right, preferred_element_type=F32)
        po_ref[...] = jnp.dot(left_odd[pl.ds(start, block), :], right, preferred_element_type=F32)
        for chunk in range(cols // LANES):
            lanes = slice(chunk * LANES, (chunk + 1) * LANES)
            bin_block(idx_ref, lanes, start, block, pe_ref, po_ref, acc_ref)
        return carry

    lax.fori_loop(0, words // block, body, 0)
    write_bins(acc_ref, out_ref, scale)


def back_kernel(block, scale, xe_ref, xo_ref, gg_ref, ug_ref, gi_ref, ui_ref, ge_ref, go_ref, ue_ref, uo_ref,
                de_ref, do_ref, gb_ref, ub_ref, acc_ref, pe_ref, po_ref):
    @pl.when(pl.program_id(0) == 0)
    def _():
        de_ref[...] = jnp.zeros_like(de_ref)
        do_ref[...] = jnp.zeros_like(do_ref)

    gate, up = gg_ref[...], ug_ref[...]
    de_ref[...] += contract_cols(gate, ge_ref[...]) + contract_cols(up, ue_ref[...])
    do_ref[...] += contract_cols(gate, go_ref[...]) + contract_cols(up, uo_ref[...])
    for grad, idx_ref, out_ref in ((gate, gi_ref, gb_ref), (up, ui_ref, ub_ref)):
        bin_columns(block, scale, xe_ref, xo_ref, grad, idx_ref, out_ref, acc_ref, pe_ref, po_ref)


def back_products(x_even, x_odd, gate_grad, up_grad, gate_index, up_index, weights, scale):
    tokens = gate_grad.shape[0]
    words, width = gate_index.shape
    cols = divisor(width, 256)
    block = math.gcd(words, 128)
    rows = pl.BlockSpec((words, tokens), lambda j: (0, 0))
    grad = pl.BlockSpec((tokens, cols), lambda j: (0, j))
    tile = pl.BlockSpec((words, cols), lambda j: (0, j))
    whole = pl.BlockSpec((tokens, words), lambda j: (0, 0))
    bins = pl.BlockSpec((16, cols), lambda j: (0, j))
    return pl.pallas_call(
        functools.partial(back_kernel, block, scale),
        grid=(width // cols,),
        in_specs=[rows, rows, grad, grad] + [tile] * 6,
        out_specs=[whole, whole, bins, bins],
        out_shape=[jax.ShapeDtypeStruct((tokens, words), F32)] * 2
        + [jax.ShapeDtypeStruct((16, width), F32)] * 2,
        scratch_shapes=[pltpu.VMEM((128, cols), F32)] + [pltpu.VMEM((block, cols), F32)] * 2,
        name="back_products",
    )(x_even.T, x_odd.T, gate_grad, up_grad, gate_index, up_index, *weights)


def bins_kernel(block, scale, ae_ref, ao_ref, og_ref, di_ref, out_ref, acc_ref, pe_ref, po_ref):
    bin_columns(block, scale, ae_ref, ao_ref, og_ref[...], di_ref, out_ref, acc_ref, pe_ref, po_ref)


def down_bins(act_even, act_odd, out_grad, down_index, scale):
    tokens = out_grad.shape[0]
    words, width = down_index.shape
    cols = divisor(width, 256)
    block = math.gcd(words, 128)
    rows = pl.BlockSpec((words, tokens), lambda j: (0, 0))
    return pl.pallas_call(
        functools.partial(bins_kernel, block, scale),
        grid=(width // cols,),
        in_specs=[
            rows,
            rows,
            pl.BlockSpec((tokens, cols), lambda j: (0, j)),
            pl.BlockSpec((words, cols), lambda j: (0, j)),
        ],
        out_specs=pl.BlockSpec((16, cols), lambda j: (0, j)),
        out_shape=jax.ShapeDtypeStruct((16, width), F32),
        scratch_shapes=[pltpu.VMEM((128, cols), F32)] + [pltpu.VMEM((block, cols), F32)] * 2,
        name="down_bins",
    )(act_even.T, act_odd.T, out_grad, down_index)


def pairing(block, dtype):
    row = jnp.arange(block)[:, None]
    col = jnp.arange(block)[None, :]
    half = block // 2
    return (row == 2 * (col % half) + col // half).astype(dtype)


def split_pairs(array):
    rows, cols = array.shape
    block = math.gcd(cols, 256)
    out = lax.dot_general(
        array.reshape(rows, cols // block, block), pairing(block, array.dtype), (((2,), (0,)), ((), ())),
        preferred_element_type=F32,
    ).astype(array.dtype)
    half = block // 2
    return out[:, :, :half].reshape(rows, cols // 2), out[:, :, half:].reshape(rows, cols // 2)


def merge_pairs(even, odd):
    rows, cols = even.shape
    block = math.gcd(2 * cols, 256)
    half = block // 2
    both = jnp.concatenate(
        [even.reshape(rows, cols // half, half), odd.reshape(rows, cols // half, half)], axis=2
    )
    return lax.dot_general(
        both, pairing(block, even.dtype), (((2,), (1,)), ((), ())), precision=lax.Precision.HIGHEST,
        preferred_element_type=F32,
    ).reshape(rows, 2 * cols)


def local_hidden(pre_gate, pre_up, hidden_grad):
    sig_gate = jax.nn.sigmoid(pre_gate)
    silu_gate = pre_gate * sig_gate
    activ = (silu_gate * pre_up).astype(BF16)
    gate_grad = (hidden_grad * pre_up * sig_gate * (1.0 + pre_gate * (1.0 - sig_gate))).astype(BF16)
    up_grad = (hidden_grad * silu_gate).astype(BF16)
    return activ, gate_grad, up_grad


def shards(inputs, out_grad, gate_index, up_index, down_index, gate_table, up_table, down_table):
    tokens = inputs.shape[0]
    width = gate_index.shape[1]
    scale = 1.0 / tokens
    x_even, x_odd = split_pairs(inputs)
    pre_gate, pre_up, *weights = up_products(x_even, x_odd, gate_index, up_index, gate_table, up_table)
    share = lax.psum_scatter(
        jnp.concatenate([pre_gate, pre_up], axis=1), "inp", scatter_dimension=0, tiled=True
    )
    hid_even, hid_odd = down_products(out_grad, down_index, down_table)
    hid = lax.psum_scatter(
        jnp.concatenate([hid_even, hid_odd], axis=1), "inp", scatter_dimension=0, tiled=True
    )
    hidden_grad = merge_pairs(hid[:, : width // 2], hid[:, width // 2 :])
    activ, gate_grad, up_grad = local_hidden(share[:, :width], share[:, width:], hidden_grad)
    act_even, act_odd = split_pairs(activ)
    grads = lax.all_gather(jnp.concatenate([gate_grad, up_grad], axis=1), "inp", axis=0, tiled=True)
    acts = lax.all_gather(jnp.concatenate([act_even, act_odd], axis=1), "inp", axis=0, tiled=True)
    din_even, din_odd, gate_bins, up_bins = back_products(
        x_even, x_odd, grads[:, :width], grads[:, width:], gate_index, up_index, weights, scale
    )
    half = din_even.shape[1]
    din = lax.psum_scatter(
        jnp.concatenate([din_even, din_odd], axis=1), "hid", scatter_dimension=0, tiled=True
    )
    input_grad = merge_pairs(din[:, :half], din[:, half:]).astype(BF16)
    gate_sum, up_sum = lax.psum((gate_bins, up_bins), "inp")
    down_sum = lax.psum(
        down_bins(acts[:, : width // 2], acts[:, width // 2 :], out_grad, down_index, scale), "hid"
    )
    return input_grad, gate_sum, up_sum, down_sum


def solution(mesh):
    in_specs = (
        P(None, "inp"),
        P(None, "inp"),
        P("inp", "hid"),
        P("inp", "hid"),
        P("hid", "inp"),
        P(None, "hid"),
        P(None, "hid"),
        P(None, "inp"),
    )
    out_specs = (P("hid", "inp"), P(None, "hid"), P(None, "hid"), P(None, "inp"))
    return jax.shard_map(shards, mesh=mesh, in_specs=in_specs, out_specs=out_specs, check_vma=False)
```

time: 2130 us -> 570 us (0.27); the launches traced: 2110 us -> 570 us
  local copies, waits for them, and re-layouts: 941 us -> 14.9 us
  other arithmetic: 758 us -> 12 us
  Pallas kernels: 0 us -> 353 us
  matrix products: 176 us -> 1.46 us
  waiting for transfers between devices: 191 us -> 165 us
    reduce_sum x183 -> x0, other arithmetic: 552 us -> none  [the longest x90 285 us: bin_block(): return jnp.sum(chosen, axis=1)]
    another operation x10 -> x0, local copies, waits for them, and re-layouts: 483 us -> none  [the longest x3 265 us: unpack(): stacked = jnp.stack(parts, axis=1)]
    pallas_call x0 -> x4, Pallas kernels: none -> 353 us  [the longest x1 168 us: back_products(): pl.pallas_call(functools.partial(back_kernel, block, scale), grid=(width...]
    eq x180 -> x0, local copies, waits for them, and re-layouts: 291 us -> none  [the longest x90 146 us: bin_block(): index_piece[None, :, :] == buckets[:, None, None]]
    another operation x6 -> x0, other arithmetic: 192 us -> none  [unpack(): stacked = jnp.stack(parts, axis=1)]
    dot_general x95 -> x4, matrix products: 176 us -> 1.46 us  [the longest x2 0.74 us: merge_pairs(): lax.dot_general(both, pairing(block, even.dtype), (((2,), (1,)), ((), ())...]
    dynamic_update_slice x180 -> x0, local copies, waits for them, and re-layouts: 155 us -> none  [the longest x90 91.1 us: decode(): pieces = lax.map(decode_block, indices.reshape(rows // block, block, cols))]
    reduce_scatter x2 -> x3, waiting for transfers between devices: 120 us -> 40.8 us  [the longest x1 40.8 us: shards(): lax.psum_scatter(jnp.concatenate([pre_gate, pre_up], axis=1), 'inp', scat...]
  transfers between devices with their start and end apart: 4 -> 6, of which waited for: 3 -> 4; matrix products, arithmetic and copies ran while one was open for 2% -> 2% of each run, Pallas kernels for 0% -> 26%
where the time goes in v1:
time: 570 us
  Pallas kernels  353 us (62%)
  waiting for transfers between devices  165 us (29%)
  local copies, waits for them, and re-layouts  14.9 us (3%)
  between operations  14.3 us (3%)
  other arithmetic  12 us (2%)
  blocking collectives  8.95 us (2%)
    pallas_call x1, Pallas kernels, back_products(): pl.pallas_call(functools.partial(back_kernel, block, scale), grid=(width...  168 us
    pallas_call x1, Pallas kernels, down_bins(): pl.pallas_call(functools.partial(bins_kernel, block, scale), grid=(width...  73.8 us
    pallas_call x1, Pallas kernels, up_products(): pl.pallas_call(functools.partial(up_kernel, block), grid=(width // cols,)...  72.9 us
    psum x1, waiting for transfers between devices, shards(): lax.psum(down_bins(acts[:, :width // 2], acts[:, width // 2:], out_grad,...  68.4 us
    reduce_scatter x1, waiting for transfers between devices, shards(): lax.psum_scatter(jnp.concatenate([pre_gate, pre_up], axis=1), 'inp', scat...  40.8 us
    pallas_call x1, Pallas kernels, down_products(): pl.pallas_call(functools.partial(down_kernel, block), grid=(width // cols...  38.3 us
    psum x1, waiting for transfers between devices, shards(): gate_sum, up_sum = lax.psum((gate_bins, up_bins), 'inp')  35 us
    all_gather x1, waiting for transfers between devices, shards(): lax.all_gather(jnp.concatenate([gate_grad, up_grad], axis=1), 'inp', axis...  20.5 us
  transfers between devices with their start and end apart: 6, of which 4 were waited for; matrix products, arithmetic and copies ran while one was open for 2% of the time, Pallas kernels for 26%

profile of v1, /device:TPU:0, one launch (start us, length us, event | category | flops | bytes accessed | tf_op | source)
XLA Modules:
  0.0 570.1 jit_solution(2667605209961807660)
XLA Ops:
  7.2 38.3 %down_products.1 = (f32[128,1664]{1,0:T(8,128)}, f32[128,1664]{1,0:T(8,128)}) custom-call(bf16[128,4096]{1,0:T(8,128)(2,1)} %og_ref.3, s32[1664,4096]{1,0:T(8,128)} %di_ref.3, f32[16,4096]{1,0:T(8,128)} %dt_ref.1), custom_call_target="tpu_custom_call" | custom-call | tf_op jit(solution)/shard_map/down_products/pallas_call | solution.py:124
  45.5 2.8 pad_maximum_fusion.2
  48.4 0.5 fusion
  48.9 0.1 fusion.29
  49.0 1.1 copy.47.xe_ref
  50.2 1.0 copy.48.xo_ref
  51.2 72.9 %up_products.1 = (f32[128,3328]{1,0:T(8,128)}, f32[128,3328]{1,0:T(8,128)}, bf16[2048,3328]{1,0:T(8,128)(2,1)}, bf16[2048,3328]{1,0:T(8,128)(2,1)}, bf16[2048,33...) custom-call(bf16[128,2048]{1,0:T(8,128)(2,1)} %copy.47.xe_ref, bf16[128,2048]{1,0:T(8,128)(2,1)} %copy.48.xo_ref, ...), custom_call_target="tpu_custom_call" | custom-call | tf_op jit(solution)/shard_map/up_products/pallas_call | solution.py:82
  124.1 4.0 pad_maximum_fusion
  128.2 1.1 slice_bitcast_fusion.1
  129.3 0.4 convolution_bitcast_fusion
  129.7 40.8 %reduce-scatter.6.cloned.1.call-done = f32[32,6656]{1,0:T(8,128)} async-done(((f32[128,6656]{1,0:T(8,128)}), f32[32,6656]{1,0:T(8,128)}) %reduce-scatter.6.cloned.1.call-update) | async-done | bytes 851984 | tf_op jit(solution)/shard_map/reduce_scatter | solution.py:298
  170.5 1.4 multiply_convert_fusion.2
  171.9 0.8 pad_maximum_fusion.3
  172.8 20.5 %all-gather.2.cloned.1.call-done = bf16[128,6656]{1,0:T(8,128)(2,1)} async-done(((bf16[32,6656]{1,0:T(8,128)(2,1)}), bf16[128,6656]{1,0:T(8,128)(2,1)}) %all-gather.2.cloned.1.call-update) | async-done | bytes 1703952 | tf_op jit(solution)/shard_map/all_gather | solution.py:308
  193.2 2.7 fusion.28
  195.9 167.8 %back_products.1 = (f32[128,2048]{1,0:T(8,128)}, f32[128,2048]{1,0:T(8,128)}, f32[16,3328]{1,0:T(8,128)}, f32[16,3328]{1,0:T(8,128)}) custom-call(bf16[2048,128]{1,0:T(8,128)(2,1)} %bitcast.59, bf16[2048,128]{1,0:T(8,128)(2,1)} %bitcast.57, bf16[128,3328]{1,0:T(8,128)(2,1)} %get-tuple-element.31.gg_ref, bf16[128,3328]{1,0:T(8,128)(2,1)} %get-tuple-element.30.ug_ref, ...), custom_call_target="tpu_custom_call" | custom-call | tf_op jit(solution)/shard_map/back_products/pallas_call | solution.py:214
  363.7 3.1 pad_maximum_fusion.1
  366.9 0.2 convolution_convert_fusion.1
  367.2 8.9 %all_gather.7 = bf16[128,3328]{1,0:T(8,128)(2,1)S(1)} all-gather(bf16[32,3328]{1,0:T(8,128)(2,1)S(1)} %pad_maximum_fusion.4), channel_id=1, replica_groups=mesh['inp'=4,'hid'=8] {'inp'}, dimensions={0}, use_global_device_ids=true | all-gather | bytes 1064960 | tf_op jit(solution)/shard_map/all_gather | solution.py:309
  376.2 0.1 fusion.30
  376.2 1.0 copy.56
  377.2 1.0 copy.57
  378.2 73.8 %down_bins.1 = f32[16,4096]{1,0:T(8,128)} custom-call(bf16[1664,128]{1,0:T(8,128)(2,1)} %bitcast.60, bf16[1664,128]{1,0:T(8,128)(2,1)} %bitcast.61, bf16[128,4096]{1,0:T(8,128)(2,1)} %og_ref.3, s32[1664,4096]{1,0:T(8,128)} %di_ref.3), custom_call_target="tpu_custom_call" | custom-call | tf_op jit(solution)/shard_map/down_bins/pallas_call | solution.py:236
  452.1 0.5 all-reduce.6.cloned.1.call-update
  452.7 1.0 slice_bitcast_fusion.3
  453.7 0.3 convolution_convert_fusion.2
  454.1 0.7 copy.67
  454.8 68.4 %all-reduce.4.cloned.1.call-done = f32[16,4096]{1,0:T(8,128)} async-done(((f32[16,4096]{1,0:T(8,128)}), f32[16,4096]{1,0:T(8,128)}) %all-reduce.4.cloned.1.call-update) | async-done | bytes 262160 | tf_op jit(solution)/shard_map/psum | solution.py:319
  523.2 35.0 %all-reduce.6.cloned.1.call-done = (f32[16,3328]{1,0:T(8,128)}, f32[16,3328]{1,0:T(8,128)}) async-done(((f32[16,3328]{1,0:T(8,128)}, f32[16,3328]{1,0:T(8,128)}), (f32[16,3328]{1,0:T(8,128)}, f32[16,3328]{1,0:T(8,128)})) %all-reduce.6.cloned.1.call-update) | async-done | bytes 426000 | tf_op jit(solution)/shard_map/psum | solution.py:318
  558.3 1.6 copy.85
  559.9 1.6 copy.86
  561.5 1.7 copy.87
  (28 shorter events, 0.6 us)
Async XLA Ops:
  7.2 121.0 %reduce-scatter.4.cloned.1.call-start = ((), (), s32[]{:S(2)}) async-start(), calls=%async_computation.3 | async-start | bytes 2129920 | tf_op jit(solution)/shard_map/reduce_scatter | solution.py:302
  45.5 2.9 copy-start.2
  48.4 122.2 %reduce-scatter.6.cloned.1.call-start = ((), (), s32[]{:S(2)}) async-start(), calls=%async_computation.4 | async-start | bytes 4259840 | tf_op jit(solution)/shard_map/reduce_scatter | solution.py:298
  49.0 75.1 %copy-start = (bf16[128,16,128]{0,2,1:T(8,128)(2,1)}, bf16[128,16,128]{0,2,1:T(8,128)(2,1)S(1)}, u32[]{:S(2)}) copy-start(bf16[128,16,128]{0,2,1:T(8,128)(2,1)S(1)} %get-tuple-element.34) | copy-start | bytes 1572868
  49.0 75.1 %copy-start.1 = (bf16[128,16,128]{0,2,1:T(8,128)(2,1)}, bf16[128,16,128]{0,2,1:T(8,128)(2,1)S(1)}, u32[]{:S(2)}) copy-start(bf16[128,16,128]{0,2,1:T(8,128)(2,1)S(1)} %get-tuple-element.35) | copy-start | bytes 1572868
  128.1 65.2 %all-gather.2.cloned.1.call-start = ((), (), s32[]{:S(2)}) async-start(), calls=%async_computation.5 | async-start | bytes 2129920 | tf_op jit(solution)/shard_map/all_gather | solution.py:308
  172.7 280.0 %reduce-scatter.8.cloned.1.call-start = ((), (), s32[]{:S(2)}) async-start(), calls=%async_computation.6 | async-start | bytes 2359296 | tf_op jit(solution)/shard_map/reduce_scatter | solution.py:314
  366.8 156.4 %all-reduce.4.cloned.1.call-start = ((), (), s32[]{:S(2)}) async-start(), calls=%async_computation.7 | async-start | bytes 524288 | tf_op jit(solution)/shard_map/psum | solution.py:319
  452.1 106.2 %all-reduce.6.cloned.1.call-start = ((), (), s32[]{:S(2)}) async-start(), calls=%async_computation.8 | async-start | bytes 851968 | tf_op jit(solution)/shard_map/psum | solution.py:318
Sparse Core Ops, SparseCore 0:
  48.5 31.5 reduce-scatter.3
  128.2 42.2 reduce-scatter.5
  172.8 20.3 all-gather.1
  366.9 68.5 reduce-scatter.7
  452.2 71.0 all-reduce.3
  526.0 32.2 all-reduce.5

commit v2 on v0

v2 whole, which is shorter than its diff:
```python
import functools
import math

import jax
import jax.numpy as jnp
from jax import lax
from jax.experimental import pallas as pl
from jax.experimental.pallas import tpu as pltpu
from jax.sharding import PartitionSpec as P

LANES = 128
SUB = 16
F32 = jnp.float32
BF16 = jnp.bfloat16


def divisor(size, most, unit=LANES):
    best = unit
    for cand in range(unit, most + 1, unit):
        if size % cand == 0:
            best = cand
    return best


def bit_masks(words, parity):
    return [(words & jnp.int16(1 << (4 * parity + bit))) != 0 for bit in range(4)]


def look_up(levels, masks):
    for mask in masks:
        levels = [jnp.where(mask, levels[i + 1], levels[i]) for i in range(0, len(levels), 2)]
    return levels[0]


def table_rows(table_ref, lanes):
    return [
        jnp.broadcast_to(table_ref[k : k + 1, lanes], (SUB, LANES)).astype(BF16)
        for k in range(16)
    ]


def pipelined(count, make, use):
    make(0, 0)

    def body(j, carry):
        make(2 * j + 1, 1)
        use(2 * j, 0)
        make(2 * j + 2, 0)
        use(2 * j + 1, 1)
        return carry

    lax.fori_loop(0, (count - 1) // 2, body, 0)
    if count % 2 == 0:
        make(count - 1, 1)
        use(count - 2, 0)
        use(count - 1, 1)
    else:
        use(count - 1, 0)


def fill_table(table_ref, rows_ref):
    cols = table_ref.shape[1]
    for chunk in range(cols // LANES):
        lanes = slice(chunk * LANES, (chunk + 1) * LANES)
        for k, row in enumerate(table_rows(table_ref, lanes)):
            rows_ref[k * SUB : (k + 1) * SUB, lanes] = row


def decode_block(idx_ref, rows_ref, i, half, store):
    cols = idx_ref.shape[1]
    for chunk in range(cols // LANES):
        lanes = slice(chunk * LANES, (chunk + 1) * LANES)
        table = [rows_ref[k * SUB : (k + 1) * SUB, lanes] for k in range(16)]
        for step in range(half // SUB):
            row = pl.multiple_of(i * half + step * SUB, SUB)
            words = idx_ref[pl.ds(row, SUB), lanes].astype(jnp.int16)
            for parity in range(2):
                store(parity * half + step * SUB, lanes, look_up(table, bit_masks(words, parity)))


def up_kernel(x_ref, idx_ref, table_ref, pre_ref, weight_ref, rows_ref, *slots):
    count, _, block = x_ref.shape
    fill_table(table_ref, rows_ref)
    pre_ref[...] = jnp.zeros_like(pre_ref)

    def make(i, slot):
        def store(row, lanes, value):
            slots[slot][row : row + SUB, lanes] = value
            weight_ref[pl.ds(pl.multiple_of(i * block + row, SUB), SUB), lanes] = value

        decode_block(idx_ref, rows_ref, i, block // 2, store)

    def use(i, slot):
        pre_ref[...] += jnp.dot(x_ref[i], slots[slot][...], preferred_element_type=F32)

    pipelined(count, make, use)


def up_product(x_blocks, index, lookup):
    count, tokens, block = x_blocks.shape
    words, width = index.shape
    cols = divisor(width, 256)
    return pl.pallas_call(
        up_kernel,
        grid=(width // cols,),
        in_specs=[
            pl.BlockSpec((count, tokens, block), lambda j: (0, 0, 0)),
            pl.BlockSpec((words, cols), lambda j: (0, j)),
            pl.BlockSpec((16, cols), lambda j: (0, j)),
        ],
        out_specs=[
            pl.BlockSpec((tokens, cols), lambda j: (0, j)),
            pl.BlockSpec((2 * words, cols), lambda j: (0, j)),
        ],
        out_shape=[
            jax.ShapeDtypeStruct((tokens, width), F32),
            jax.ShapeDtypeStruct((2 * words, width), BF16),
        ],
        scratch_shapes=[pltpu.VMEM((16 * SUB, cols), BF16)] + [pltpu.VMEM((block, cols), BF16)] * 2,
        name="up_product",
    )(x_blocks, index, lookup)


def down_kernel(og_ref, idx_ref, table_ref, out_ref, rows_ref, *slots):
    count, _, block = out_ref.shape
    fill_table(table_ref, rows_ref)

    @pl.when(pl.program_id(0) == 0)
    def _():
        out_ref[...] = jnp.zeros_like(out_ref)

    def make(i, slot):
        def store(row, lanes, value):
            slots[slot][row : row + SUB, lanes] = value

        decode_block(idx_ref, rows_ref, i, block // 2, store)

    def use(i, slot):
        out_ref[i] += contract_cols(og_ref[...], slots[slot][...])

    pipelined(count, make, use)


def down_product(out_grad, index, lookup):
    tokens = out_grad.shape[0]
    words, width = index.shape
    cols = divisor(width, 256)
    block = math.gcd(2 * words, 256)
    count = 2 * words // block
    return pl.pallas_call(
        down_kernel,
        grid=(width // cols,),
        in_specs=[
            pl.BlockSpec((tokens, cols), lambda j: (0, j)),
            pl.BlockSpec((words, cols), lambda j: (0, j)),
            pl.BlockSpec((16, cols), lambda j: (0, j)),
        ],
        out_specs=pl.BlockSpec((count, tokens, block), lambda j: (0, 0, 0)),
        out_shape=jax.ShapeDtypeStruct((count, tokens, block), F32),
        scratch_shapes=[pltpu.VMEM((16 * SUB, cols), BF16)] + [pltpu.VMEM((block, cols), BF16)] * 2,
        name="down_product",
    )(out_grad, index, lookup)


def contract_cols(left, right):
    return lax.dot_general(left, right, (((1,), (1,)), ((), ())), preferred_element_type=F32)


def input_kernel(gate_ref, up_ref, wg_ref, wu_ref, out_ref):
    count, _, block = out_ref.shape

    @pl.when(pl.program_id(0) == 0)
    def _():
        out_ref[...] = jnp.zeros_like(out_ref)

    gate, up = gate_ref[...], up_ref[...]

    def body(i, carry):
        rows = pl.ds(pl.multiple_of(i * block, block), block)
        out_ref[i] += contract_cols(gate, wg_ref[rows, :]) + contract_cols(up, wu_ref[rows, :])
        return carry

    lax.fori_loop(0, count, body, 0, unroll=2 if count % 2 == 0 else 1)


def input_product(gate_grad, up_grad, w_gate, w_up):
    tokens, width = gate_grad.shape
    rows = w_gate.shape[0]
    cols = divisor(width, 256)
    block = math.gcd(rows, 256)
    grad = pl.BlockSpec((tokens, cols), lambda j: (0, j))
    weight = pl.BlockSpec((rows, cols), lambda j: (0, j))
    return pl.pallas_call(
        input_kernel,
        grid=(width // cols,),
        in_specs=[grad, grad, weight, weight],
        out_specs=pl.BlockSpec((rows // block, tokens, block), lambda j: (0, 0, 0)),
        out_shape=jax.ShapeDtypeStruct((rows // block, tokens, block), F32),
        name="input_product",
    )(gate_grad, up_grad, w_gate, w_up)


def leaves(value, masks):
    b0, b1, b2, b3 = masks
    zero = jnp.zeros_like(value)
    out = []
    for part in (jnp.where(b3, zero, value), jnp.where(b3, value, zero)):
        for piece in (jnp.where(b2, zero, part), jnp.where(b2, part, zero)):
            one = jnp.where(b1, piece, zero)
            out += [piece, jnp.where(b0, piece, zero), one, jnp.where(b0, one, zero)]
    return out


def write_bins(acc_ref, out_ref, scale):
    rows = [jnp.sum(acc_ref[8 * k : 8 * k + 8, :], axis=0, keepdims=True) for k in range(16)]
    for k in range(0, 16, 4):
        none, low, high, both = rows[k : k + 4]
        out_ref[k : k + 1, :] = ((none - low) - (high - both)) * scale
        out_ref[k + 1 : k + 2, :] = (low - both) * scale
        out_ref[k + 2 : k + 3, :] = (high - both) * scale
        out_ref[k + 3 : k + 4, :] = both * scale


def bins_kernel(scale, left_ref, right_ref, idx_ref, out_ref, acc_ref, *slots):
    count, block, _ = left_ref.shape
    half = block // 2
    cols = idx_ref.shape[1]
    acc_ref[...] = jnp.zeros_like(acc_ref)

    def make(i, slot):
        slots[slot][...] = jnp.dot(left_ref[i], right_ref[...], preferred_element_type=F32).astype(BF16)

    def use(i, slot):
        for chunk in range(cols // LANES):
            lanes = slice(chunk * LANES, (chunk + 1) * LANES)
            sums = None
            for step in range(half // SUB):
                row = pl.multiple_of(i * half + step * SUB, SUB)
                words = idx_ref[pl.ds(row, SUB), lanes].astype(jnp.int16)
                for parity in range(2):
                    first = parity * half + step * SUB
                    parts = leaves(slots[slot][first : first + SUB, lanes], bit_masks(words, parity))
                    sums = parts if sums is None else [a + b for a, b in zip(sums, parts)]
            for k, total in enumerate(sums):
                wide = total.astype(F32)
                acc_ref[8 * k : 8 * k + 8, lanes] += wide[:8] + wide[8:]

    pipelined(count, make, use)
    write_bins(acc_ref, out_ref, scale)


def bins(left_blocks, right, index, scale):
    count, tokens, block = left_blocks.shape
    words, width = index.shape
    cols = divisor(width, 256)
    return pl.pallas_call(
        functools.partial(bins_kernel, scale),
        grid=(width // cols,),
        in_specs=[
            pl.BlockSpec((count, block, tokens), lambda j: (0, 0, 0)),
            pl.BlockSpec((tokens, cols), lambda j: (0, j)),
            pl.BlockSpec((words, cols), lambda j: (0, j)),
        ],
        out_specs=pl.BlockSpec((16, cols), lambda j: (0, j)),
        out_shape=jax.ShapeDtypeStruct((16, width), F32),
        scratch_shapes=[pltpu.VMEM((128, cols), F32)] + [pltpu.VMEM((block, cols), BF16)] * 2,
        name="bins",
    )(jnp.swapaxes(left_blocks, 1, 2), right, index)


def pairing(block, dtype):
    row = jnp.arange(block)[:, None]
    col = jnp.arange(block)[None, :]
    half = block // 2
    return (row == 2 * (col % half) + col // half).astype(dtype)


def to_blocks(array):
    rows, cols = array.shape
    block = math.gcd(cols, 256)
    out = lax.dot_general(
        array.reshape(rows, cols // block, block), pairing(block, array.dtype), (((2,), (0,)), ((), ())),
        preferred_element_type=F32,
    )
    return jnp.swapaxes(out.astype(array.dtype), 0, 1)


def from_blocks(blocks):
    count, rows, block = blocks.shape
    out = lax.dot_general(
        blocks, pairing(block, blocks.dtype), (((2,), (1,)), ((), ())), precision=lax.Precision.HIGHEST,
        preferred_element_type=F32,
    )
    return jnp.swapaxes(out, 0, 1).reshape(rows, count * block)


def exchange(array, axis, size, bit):
    return lax.ppermute(array, axis, [(i, i ^ bit) for i in range(size)])


def axis_bits(size):
    return [1 << i for i in range(size.bit_length() - 1)]


def sum_scatter(array, axis):
    size = lax.axis_size(axis)
    if size & (size - 1):
        return lax.psum_scatter(array, axis, scatter_dimension=0, tiled=True)
    me = lax.axis_index(axis)
    rows, cols = array.shape
    array = array.reshape(size, rows // size, cols)
    for bit in axis_bits(size):
        pairs = array.reshape(array.shape[0] // 2, 2, rows // size, cols)
        mine = jnp.bitwise_and(me // bit, 1)
        sent = exchange(lax.dynamic_index_in_dim(pairs, 1 - mine, 1, False), axis, size, bit)
        array = lax.dynamic_index_in_dim(pairs, mine, 1, False) + sent
    return array.reshape(rows // size, cols)


def gather(array, axis):
    size = lax.axis_size(axis)
    if size & (size - 1):
        return lax.all_gather(array, axis, axis=0, tiled=True)
    me = lax.axis_index(axis)
    rows, cols = array.shape
    array = array[None]
    for bit in reversed(axis_bits(size)):
        other = exchange(array, axis, size, bit)
        first = jnp.bitwise_and(me // bit, 1) == 0
        low, high = jnp.where(first, array, other), jnp.where(first, other, array)
        array = jnp.stack([low, high], axis=1).reshape(-1, rows, cols)
    return array.reshape(size * rows, cols)


def sum_all(array, axis):
    size = lax.axis_size(axis)
    if size & (size - 1):
        return lax.psum(array, axis)
    for bit in axis_bits(size):
        array = array + exchange(array, axis, size, bit)
    return array


def after(array, *done):
    return lax.optimization_barrier((array, *done))[0]


def local_hidden(pre_gate, pre_up, hidden_grad):
    sig_gate = jax.nn.sigmoid(pre_gate)
    silu_gate = pre_gate * sig_gate
    activ = (silu_gate * pre_up).astype(BF16)
    gate_grad = (hidden_grad * pre_up * sig_gate * (1.0 + pre_gate * (1.0 - sig_gate))).astype(BF16)
    up_grad = (hidden_grad * silu_gate).astype(BF16)
    return activ, gate_grad, up_grad


def shards(inputs, out_grad, gate_index, up_index, down_index, gate_table, up_table, down_table):
    tokens = inputs.shape[0]
    width = gate_index.shape[1]
    scale = 1.0 / tokens
    hid_blocks = down_product(out_grad, down_index, down_table)
    count, _, block = hid_blocks.shape
    hid = lax.psum_scatter(hid_blocks, "inp", scatter_dimension=1, tiled=True)
    x_blocks = to_blocks(inputs)
    pre_gate, w_gate = up_product(x_blocks, gate_index, after(gate_table, hid_blocks))
    gate_share = lax.psum_scatter(pre_gate, "inp", scatter_dimension=0, tiled=True)
    pre_up, w_up = up_product(x_blocks, up_index, after(up_table, pre_gate))
    up_share = sum_scatter(pre_up, "inp")
    activ, gate_grad, up_grad = local_hidden(gate_share, up_share, from_blocks(hid))
    grads = gather(jnp.concatenate([gate_grad, up_grad], axis=1), "inp")
    gate_grad, up_grad = grads[:, :width], grads[:, width:]
    acts = gather(after(activ, gate_grad), "inp")
    din_blocks = input_product(gate_grad, up_grad, w_gate, w_up)
    din = lax.psum_scatter(din_blocks, "hid", scatter_dimension=1, tiled=True)
    input_grad = from_blocks(din).astype(BF16)
    act_blocks = to_blocks(after(acts, din_blocks))
    down_part = bins(act_blocks, out_grad, down_index, scale)
    down_sum = lax.psum(after(down_part, din), "hid")
    gate_part = bins(x_blocks, after(gate_grad, down_part, din), gate_index, scale)
    up_part = bins(x_blocks, after(up_grad, gate_part, down_sum), up_index, scale)
    up_width = up_part.shape[1]
    sums = sum_all(jnp.concatenate([gate_part, up_part], axis=1), "inp")
    gate_sum, up_sum = sums[:, :up_width], sums[:, up_width:]
    return input_grad, gate_sum, up_sum, down_sum


def solution(mesh):
    in_specs = (
        P(None, "inp"),
        P(None, "inp"),
        P("inp", "hid"),
        P("inp", "hid"),
        P("hid", "inp"),
        P(None, "hid"),
        P(None, "hid"),
        P(None, "inp"),
    )
    out_specs = (P("hid", "inp"), P(None, "hid"), P(None, "hid"), P(None, "inp"))
    return jax.shard_map(shards, mesh=mesh, in_specs=in_specs, out_specs=out_specs, check_vma=False)
```

time: 2130 us -> 468 us (0.22)
  local copies, waits for them, and re-layouts: 941 us -> 8.1 us
  other arithmetic: 758 us -> 4.14 us
  Pallas kernels: 0 us -> 379 us
  matrix products: 176 us -> 3.61 us
  waiting for transfers between devices: 191 us -> 49.7 us
  blocking collectives: 26.9 us -> 0 us
    reduce_sum x183 -> x0, other arithmetic: 552 us -> none  [the longest x90 285 us: bin_block(): return jnp.sum(chosen, axis=1)]
    another operation x10 -> x2, local copies, waits for them, and re-layouts: 483 us -> 0.17 us  [gather(): array = jnp.stack([low, high], axis=1).reshape(-1, rows, cols)]
    pallas_call x0 -> x7, Pallas kernels: none -> 379 us  [the longest x3 191 us: bins(): pl.pallas_call(functools.partial(bins_kernel, scale), grid=(width // cols...]
    eq x180 -> x0, local copies, waits for them, and re-layouts: 291 us -> none  [the longest x90 146 us: bin_block(): index_piece[None, :, :] == buckets[:, None, None]]
    another operation x6, other arithmetic: 192 us -> 0.61 us  [gather(): array = jnp.stack([low, high], axis=1).reshape(-1, rows, cols)]
    dot_general x95 -> x4, matrix products: 176 us -> 3.61 us  [the longest x2 1.87 us: to_blocks(): lax.dot_general(array.reshape(rows, cols // block, block), pairing(block,...]
    dynamic_update_slice x180 -> x0, local copies, waits for them, and re-layouts: 155 us -> none  [the longest x90 91.1 us: decode(): pieces = lax.map(decode_block, indices.reshape(rows // block, block, cols))]
    reduce_scatter x2 -> x3, waiting for transfers between devices: 120 us -> 0.01 us  [the longest x1 0.01 us: shards(): hid = lax.psum_scatter(hid_blocks, 'inp', scatter_dimension=1, tiled=True)]
  transfers between devices with their start and end apart: 4 -> 12, of which waited for: 3 -> 9; matrix products, arithmetic and copies ran while one was open for 2% -> 2% of each run, Pallas kernels for 0% -> 49%
where the time goes in v2:
time: 468 us; the launch traced here: 467 us
  Pallas kernels  379 us (81%)
  waiting for transfers between devices  49.7 us (11%)
  between operations  14 us (3%)
  starting transfers between devices  8.74 us (2%)
  local copies, waits for them, and re-layouts  8.1 us (2%)
    pallas_call x3, Pallas kernels, bins(): pl.pallas_call(functools.partial(bins_kernel, scale), grid=(width // cols...  191 us
    pallas_call x2, Pallas kernels, up_product(): pl.pallas_call(up_kernel, grid=(width // cols,), in_specs=[pl.BlockSpec((...  102 us
    pallas_call x1, Pallas kernels, down_product(): pl.pallas_call(down_kernel, grid=(width // cols,), in_specs=[pl.BlockSpec...  49 us
    ppermute x8, waiting for transfers between devices, exchange(): return lax.ppermute(array, axis, [(i, i ^ bit) for i in range(size)])  41.3 us
    pallas_call x1, Pallas kernels, input_product(): pl.pallas_call(input_kernel, grid=(width // cols,), in_specs=[grad, grad,...  36.6 us
  transfers between devices with their start and end apart: 12, of which 9 were waited for; matrix products, arithmetic and copies ran while one was open for 2% of the time, Pallas kernels for 49%

profile of v2, /device:TPU:0, one launch (start us, length us, event | category | flops | bytes accessed | tf_op | source)
XLA Modules:
  0.0 467.5 jit_solution(9214318857341701074)
XLA Ops:
  7.2 49.0 %down_product.1 = f32[13,128,256]{2,1,0:T(8,128)} custom-call(bf16[128,4096]{1,0:T(8,128)(2,1)} %right_ref.1, s32[1664,4096]{1,0:T(8,128)} %idx_ref.9, f32[16,4096]{1,0:T(8,128)} %table_ref.1), custom_call_target="tpu_custom_call" | custom-call | tf_op jit(solution)/shard_map/down_product/pallas_call | solution.py:150
  56.3 1.1 copy-done.3
  57.9 1.3 copy.23.x_ref
  59.2 51.1 %up_product.2 = (f32[128,3328]{1,0:T(8,128)}, bf16[4096,3328]{1,0:T(8,128)(2,1)}) custom-call(bf16[16,128,256]{2,1,0:T(8,128)(2,1)} %copy.23.x_ref, s32[2048,3328]{1,0:T(8,128)} %idx_ref.10, f32[16,3328]{1,0:T(8,128)} %table_ref.2), custom_call_target="tpu_custom_call" | custom-call | tf_op jit(solution)/shard_map/up_product/pallas_call | solution.py:103
  110.4 51.1 %up_product.3 = (f32[128,3328]{1,0:T(8,128)}, bf16[4096,3328]{1,0:T(8,128)(2,1)}) custom-call(bf16[16,128,256]{2,1,0:T(8,128)(2,1)} %copy.23.x_ref, s32[2048,3328]{1,0:T(8,128)} %idx_ref.11, f32[16,3328]{1,0:T(8,128)} %table_ref.3), custom_call_target="tpu_custom_call" | custom-call | tf_op jit(solution)/shard_map/up_product/pallas_call | solution.py:103
  161.5 1.3 dynamic-slice_bitcast_fusion
  163.4 2.0 collective-permute-done
  165.6 2.9 collective-permute-start.1
  168.5 1.4 convolution_bitcast_fusion
  170.0 8.7 %collective-permute-done.1 = f32[1,32,3328]{2,1,0:T(8,128)S(1)} collective-permute-done((f32[1,32,3328]{2,1,0:T(8,128)S(1)}, f32[1,32,3328]{2,1,0:T(8,128)S(1)}, u32[]{:S(2)}, u32[]{:S(2)}) %collective-permute-start.1) | collective-permute-done | bytes 426016 | tf_op jit(solution)/shard_map/ppermute | solution.py:298
  178.7 1.2 fusion.7
  179.9 1.8 collective-permute-start.2
  181.7 9.5 %collective-permute-done.2 = bf16[1,32,6656]{2,1,0:T(8,128)(2,1)S(1)} collective-permute-done((bf16[1,32,6656]{2,1,0:T(8,128)(2,1)S(1)}, bf16[1,32,6656]{2,1,0:T(8,128)(2,1)S(1)}, u32[]{:S(2)}, u32[]{:S(2)}) %collective-permute-start.2) | collective-permute-done | bytes 426016 | tf_op jit(solution)/shard_map/ppermute | solution.py:298
  191.6 2.4 collective-permute-done.3
  194.4 1.3 fusion.24
  195.7 36.6 %input_product.1 = f32[16,128,256]{2,1,0:T(8,128)} custom-call(bf16[128,3328]{1,0:T(8,128)(2,1)} %get-tuple-element.23.gate_ref.right_ref, bf16[128,3328]{1,0:T(8,128)(2,1)} %get-tuple-element.25.up_ref.right_ref, bf16[4096,3328]{1,0:T(8,128)(2,1)} %get-tuple-element.19.wg_ref, bf16[4096,3328]{1,0:T(8,128)(2,1)} %get-tuple-element.20.wu_ref), custom_call_target="tpu_custom_call" | custom-call | tf_op jit(solution)/shard_map/input_product/pallas_call | solution.py:193
  232.3 1.5 collective-permute-start.4
  233.8 5.8 %collective-permute-done.4 = bf16[1,32,3328]{2,1,0:T(8,128)(2,1)S(1)} collective-permute-done((bf16[1,32,3328]{2,1,0:T(8,128)(2,1)S(1)}, bf16[1,32,3328]{2,1,0:T(8,128)(2,1)S(1)}, u32[]{:S(2)}, u32[]{:S(2)}) %collective-permute-start.4) | collective-permute-done | bytes 213024 | tf_op jit(solution)/shard_map/ppermute | solution.py:298
  239.9 1.8 collective-permute-done.5
  242.4 1.4 fusion.left_ref
  243.8 63.3 %bins.3 = f32[16,4096]{1,0:T(8,128)} custom-call(bf16[13,256,128]{2,1,0:T(8,128)(2,1)} %fusion.left_ref, bf16[128,4096]{1,0:T(8,128)(2,1)} %right_ref.1, s32[1664,4096]{1,0:T(8,128)} %idx_ref.9), custom_call_target="tpu_custom_call" | custom-call | tf_op jit(solution)/shard_map/bins/pallas_call | solution.py:256
  307.1 64.1 %bins.4 = f32[16,3328]{1,0:T(8,128)} custom-call(bf16[16,256,128]{2,1,0:T(8,128)(2,1)} %bitcast.85, bf16[128,3328]{1,0:T(8,128)(2,1)} %get-tuple-element.23.gate_ref.right_ref, s32[2048,3328]{1,0:T(8,128)} %idx_ref.10), custom_call_target="tpu_custom_call" | custom-call | tf_op jit(solution)/shard_map/bins/pallas_call | solution.py:256
  371.2 8.4 %all-reduce.2.cloned.1.call-done = f32[16,4096]{1,0:T(8,128)} async-done(((f32[16,4096]{1,0:T(8,128)}), f32[16,4096]{1,0:T(8,128)}) %all-reduce.2.cloned.1.call-update) | async-done | bytes 262160 | tf_op jit(solution)/shard_map/psum | solution.py:378
  379.6 64.0 %bins.5 = f32[16,3328]{1,0:T(8,128)} custom-call(bf16[16,256,128]{2,1,0:T(8,128)(2,1)} %bitcast.86, bf16[128,3328]{1,0:T(8,128)(2,1)} %get-tuple-element.25.up_ref.right_ref, s32[2048,3328]{1,0:T(8,128)} %idx_ref.11), custom_call_target="tpu_custom_call" | custom-call | tf_op jit(solution)/shard_map/bins/pallas_call | solution.py:256
  443.6 1.0 pad_maximum_fusion.2
  444.7 1.8 collective-permute-done.6
  446.5 1.0 fusion.23
  447.5 1.5 collective-permute-start.7
  449.4 0.7 copy.36
  450.0 9.4 %collective-permute-done.7 = f32[16,6656]{1,0:T(8,128)S(1)} collective-permute-done((f32[16,6656]{1,0:T(8,128)S(1)}, f32[16,6656]{1,0:T(8,128)S(1)}, u32[]{:S(2)}, u32[]{:S(2)}) %collective-permute-start.7) | collective-permute-done | bytes 426016 | tf_op jit(solution)/shard_map/ppermute | solution.py:298
  459.4 0.8 fusion.25
  460.2 0.7 copy.42
  (45 shorter events, 3.6 us)
Async XLA Ops:
  7.2 161.4 %reduce-scatter.4.cloned.1.call-start = ((), (), s32[]{:S(2)}) async-start(), calls=%async_computation.3 | async-start | bytes 2129920 | tf_op jit(solution)/shard_map/reduce_scatter | solution.py:363
  56.2 1.2 copy-start.3
  56.2 122.4 %reduce-scatter.6.cloned.1.call-start = ((), (), s32[]{:S(2)}) async-start(), calls=%async_computation.4 | async-start | bytes 2129920 | tf_op jit(solution)/shard_map/reduce_scatter | solution.py:366
  57.9 52.4 %copy-start = (bf16[256,128,16]{1,0,2:T(8,128)(2,1)}, bf16[256,128,16]{1,0,2:T(8,128)(2,1)S(1)}, u32[]{:S(2)}) copy-start(bf16[256,128,16]{1,0,2:T(8,128)(2,1)S(1)} %convolution_convert_fusion) | copy-start | bytes 3145732
  110.4 196.7 %reduce-scatter.8.cloned.1.call-start = ((), (), s32[]{:S(2)}) async-start(), calls=%async_computation.5 | async-start | bytes 2359296 | tf_op jit(solution)/shard_map/reduce_scatter | solution.py:374
  161.5 3.9 copy-start.2
  162.9 2.6 collective-permute-start
  165.6 13.1 %collective-permute-start.1 = (f32[1,32,3328]{2,1,0:T(8,128)S(1)}, f32[1,32,3328]{2,1,0:T(8,128)S(1)}, u32[]{:S(2)}, u32[]{:S(2)}) collective-permute-start(f32[1,32,3328]{2,1,0:T(8,128)S(1)} %constant_dynamic-slice_fusion), channel_id=1, source_target_pairs={{0,16},{8,24},{16,0},{24,8},{1,17},{9,25},{17,1},{25,9},{2,18},{10... | collective-permute-start | bytes 1277960 | tf_op jit(solution)/shard_map/ppermute | solution.py:298
  179.9 11.3 %collective-permute-start.2 = (bf16[1,32,6656]{2,1,0:T(8,128)(2,1)S(1)}, bf16[1,32,6656]{2,1,0:T(8,128)(2,1)S(1)}, u32[]{:S(2)}, u32[]{:S(2)}) collective-permute-start(bf16[1,32,6656]{2,1,0:T(8,128)(2,1)S(1)} %maximum_bitcast_fusion.1), channel_id=1, source_target_pairs={{0,16},{8,24},{16,0},{24,8},{1,17},{9,25},{17,1},{25,9},{2,18},{10... | collective-permute-start | bytes 1277960 | tf_op jit(solution)/shard_map/ppermute | solution.py:298
  191.5 2.4 collective-permute-start.3
  232.3 147.3 %all-reduce.2.cloned.1.call-start = ((), (), s32[]{:S(2)}) async-start(), calls=%async_computation.6 | async-start | bytes 524288 | tf_op jit(solution)/shard_map/psum | solution.py:378
  232.3 7.4 %collective-permute-start.4 = (bf16[1,32,3328]{2,1,0:T(8,128)(2,1)S(1)}, bf16[1,32,3328]{2,1,0:T(8,128)(2,1)S(1)}, u32[]{:S(2)}, u32[]{:S(2)}) collective-permute-start(bf16[1,32,3328]{2,1,0:T(8,128)(2,1)S(1)} %bitcast.94), channel_id=1, source_target_pairs={{0,16},{8,24},{16,0},{24,8},{1,17},{9,25},{17,1},{25,9},{2,18},{10... | collective-permute-start | bytes 638984 | tf_op jit(solution)/shard_map/ppermute | solution.py:298
  239.8 1.8 collective-permute-start.5
  371.2 72.4 %copy-start.1 = (f32[16,3328]{1,0:T(8,128)S(1)}, f32[16,3328]{1,0:T(8,128)}, u32[]{:S(2)}) copy-start(f32[16,3328]{1,0:T(8,128)} %bins.4) | copy-start | bytes 638980
  443.6 5.4 %copy-start.4 = (f32[16,16,256]{2,1,0:T(8,128)S(1)}, f32[16,16,256]{2,1,0:T(8,128)}, u32[]{:S(2)}) copy-start(f32[16,16,256]{2,1,0:T(8,128)} %reduce-scatter.8.cloned.1.call-done) | copy-start | bytes 786436
  444.6 1.8 collective-permute-start.6
  447.5 12.8 %copy-start.5 = (f32[16,4096]{1,0:T(8,128)S(1)}, f32[16,4096]{1,0:T(8,128)}, u32[]{:S(2)}) copy-start(f32[16,4096]{1,0:T(8,128)} %all-reduce.2.cloned.1.call-done) | copy-start | bytes 786436
  447.5 11.9 %collective-permute-start.7 = (f32[16,6656]{1,0:T(8,128)S(1)}, f32[16,6656]{1,0:T(8,128)S(1)}, u32[]{:S(2)}, u32[]{:S(2)}) collective-permute-start(f32[16,6656]{1,0:T(8,128)S(1)} %fusion.23), channel_id=1, source_target_pairs={{0,16},{8,24},{16,0},{24,8},{1,17},{9,25},{17,1},{25,9},{2,18},{10... | collective-permute-start | bytes 1277960 | tf_op jit(solution)/shard_map/ppermute | solution.py:298
Sparse Core Ops, SparseCore 0:
  56.3 31.5 reduce-scatter.3
  110.5 31.5 reduce-scatter.5
  232.4 70.6 reduce-scatter.7
  307.3 72.2 all-reduce.1

commit v3 on v2

--- a/solution.py
+++ b/solution.py
@@ -58,42 +58,30 @@
         use(count - 1, 0)
 
 
-def fill_table(table_ref, rows_ref):
-    cols = table_ref.shape[1]
+def decode_tile(idx_ref, table_ref, weight_ref, half):
+    words, cols = idx_ref.shape
     for chunk in range(cols // LANES):
         lanes = slice(chunk * LANES, (chunk + 1) * LANES)
-        for k, row in enumerate(table_rows(table_ref, lanes)):
-            rows_ref[k * SUB : (k + 1) * SUB, lanes] = row
-
-
-def decode_block(idx_ref, rows_ref, i, half, store):
-    cols = idx_ref.shape[1]
-    for chunk in range(cols // LANES):
-        lanes = slice(chunk * LANES, (chunk + 1) * LANES)
-        table = [rows_ref[k * SUB : (k + 1) * SUB, lanes] for k in range(16)]
-        for step in range(half // SUB):
-            row = pl.multiple_of(i * half + step * SUB, SUB)
-            words = idx_ref[pl.ds(row, SUB), lanes].astype(jnp.int16)
-            for parity in range(2):
-                store(parity * half + step * SUB, lanes, look_up(table, bit_masks(words, parity)))
-
-
-def up_kernel(x_ref, idx_ref, table_ref, pre_ref, weight_ref, rows_ref, *slots):
+        table = table_rows(table_ref, lanes)
+
+        def body(i, carry):
+            for step in range(half // SUB):
+                piece = idx_ref[pl.ds(pl.multiple_of(i * half + step * SUB, SUB), SUB), lanes].astype(jnp.int16)
+                for parity in range(2):
+                    row = pl.multiple_of((2 * i + parity) * half + step * SUB, SUB)
+                    weight_ref[pl.ds(row, SUB), lanes] = look_up(table, bit_masks(piece, parity))
+            return carry
+
+        lax.fori_loop(0, words // half, body, 0)
+
+
+def up_kernel(x_ref, idx_ref, table_ref, pre_ref, weight_ref):
     count, _, block = x_ref.shape
-    fill_table(table_ref, rows_ref)
-    pre_ref[...] = jnp.zeros_like(pre_ref)
-
-    def make(i, slot):
-        def store(row, lanes, value):
-            slots[slot][row : row + SUB, lanes] = value
-            weight_ref[pl.ds(pl.multiple_of(i * block + row, SUB), SUB), lanes] = value
-
-        decode_block(idx_ref, rows_ref, i, block // 2, store)
-
-    def use(i, slot):
-        pre_ref[...] += jnp.dot(x_ref[i], slots[slot][...], preferred_element_type=F32)
-
-    pipelined(count, make, use)
+    decode_tile(idx_ref, table_ref, weight_ref, block // 2)
+    pre_ref[...] = sum(
+        jnp.dot(x_ref[i], weight_ref[i * block : (i + 1) * block, :], preferred_element_type=F32)
+        for i in range(count)
+    )
 
 
 def up_product(x_blocks, index, lookup):
@@ -116,29 +104,20 @@
             jax.ShapeDtypeStruct((tokens, width), F32),
             jax.ShapeDtypeStruct((2 * words, width), BF16),
         ],
-        scratch_shapes=[pltpu.VMEM((16 * SUB, cols), BF16)] + [pltpu.VMEM((block, cols), BF16)] * 2,
         name="up_product",
     )(x_blocks, index, lookup)
 
 
-def down_kernel(og_ref, idx_ref, table_ref, out_ref, rows_ref, *slots):
+def down_kernel(og_ref, idx_ref, table_ref, out_ref, weight_ref):
     count, _, block = out_ref.shape
-    fill_table(table_ref, rows_ref)
 
     @pl.when(pl.program_id(0) == 0)
     def _():
         out_ref[...] = jnp.zeros_like(out_ref)
 
-    def make(i, slot):
-        def store(row, lanes, value):
-            slots[slot][row : row + SUB, lanes] = value
-
-        decode_block(idx_ref, rows_ref, i, block // 2, store)
-
-    def use(i, slot):
-        out_ref[i] += contract_cols(og_ref[...], slots[slot][...])
-
-    pipelined(count, make, use)
+    decode_tile(idx_ref, table_ref, weight_ref, block // 2)
+    for i in range(count):
+        out_ref[i] += contract_cols(og_ref[...], weight_ref[i * block : (i + 1) * block, :])
 
 
 def down_product(out_grad, index, lookup):
@@ -157,7 +136,7 @@
         ],
         out_specs=pl.BlockSpec((count, tokens, block), lambda j: (0, 0, 0)),
         out_shape=jax.ShapeDtypeStruct((count, tokens, block), F32),
-        scratch_shapes=[pltpu.VMEM((16 * SUB, cols), BF16)] + [pltpu.VMEM((block, cols), BF16)] * 2,
+        scratch_shapes=[pltpu.VMEM((2 * words, cols), BF16)],
         name="down_product",
     )(out_grad, index, lookup)
 

time: 468 us -> 428 us (0.915)
  Pallas kernels: 379 us -> 339 us
    pallas_call x2, Pallas kernels: 102 us -> 70.8 us  [up_product(): pl.pallas_call(up_kernel, grid=(width // cols,), in_specs=[pl.BlockSpec((...]
    pallas_call x1, Pallas kernels: 49 us -> 40.7 us  [down_product(): pl.pallas_call(down_kernel, grid=(width // cols,), in_specs=[pl.BlockSpec...]
  transfers between devices with their start and end apart: 12 -> 12, of which waited for: 9 -> 9; matrix products, arithmetic and copies ran while one was open for 2% -> 2% of each run, Pallas kernels for 49% -> 46%
where the time goes in v3:
time: 428 us
  Pallas kernels  339 us (79%)
  waiting for transfers between devices  49.7 us (12%)
  between operations  14 us (3%)
  starting transfers between devices  8.75 us (2%)
  local copies, waits for them, and re-layouts  8.1 us (2%)
    pallas_call x3, Pallas kernels, bins(): pl.pallas_call(functools.partial(bins_kernel, scale), grid=(width // cols...  191 us
    pallas_call x2, Pallas kernels, up_product(): pl.pallas_call(up_kernel, grid=(width // cols,), in_specs=[pl.BlockSpec((...  70.8 us
    ppermute x8, waiting for transfers between devices, exchange(): return lax.ppermute(array, axis, [(i, i ^ bit) for i in range(size)])  41.3 us
    pallas_call x1, Pallas kernels, down_product(): pl.pallas_call(down_kernel, grid=(width // cols,), in_specs=[pl.BlockSpec...  40.7 us
    pallas_call x1, Pallas kernels, input_product(): pl.pallas_call(input_kernel, grid=(width // cols,), in_specs=[grad, grad,...  36.6 us
    ppermute x8, starting transfers between devices, exchange(): return lax.ppermute(array, axis, [(i, i ^ bit) for i in range(size)])  8.58 us
  transfers between devices with their start and end apart: 12, of which 9 were waited for; matrix products, arithmetic and copies ran while one was open for 2% of the time, Pallas kernels for 46%

profile of v3, /device:TPU:0, one launch (start us, length us, event | category | flops | bytes accessed | tf_op | source)
XLA Modules:
  0.0 427.8 jit_solution(3384131667653121954)
XLA Ops:
  7.2 40.7 %down_product.1 = f32[13,128,256]{2,1,0:T(8,128)} custom-call(bf16[128,4096]{1,0:T(8,128)(2,1)} %right_ref.1, s32[1664,4096]{1,0:T(8,128)} %idx_ref.9, f32[16,4096]{1,0:T(8,128)} %table_ref.1), custom_call_target="tpu_custom_call" | custom-call | tf_op jit(solution)/shard_map/down_product/pallas_call | solution.py:129
  48.0 1.1 copy-done.3
  49.7 1.3 copy.23.x_ref
  51.0 35.4 %up_product.2 = (f32[128,3328]{1,0:T(8,128)}, bf16[4096,3328]{1,0:T(8,128)(2,1)}) custom-call(bf16[16,128,256]{2,1,0:T(8,128)(2,1)} %copy.23.x_ref, s32[2048,3328]{1,0:T(8,128)} %idx_ref.10, f32[16,3328]{1,0:T(8,128)} %table_ref.2), custom_call_target="tpu_custom_call" | custom-call | tf_op jit(solution)/shard_map/up_product/pallas_call | solution.py:91
  86.5 35.4 %up_product.3 = (f32[128,3328]{1,0:T(8,128)}, bf16[4096,3328]{1,0:T(8,128)(2,1)}) custom-call(bf16[16,128,256]{2,1,0:T(8,128)(2,1)} %copy.23.x_ref, s32[2048,3328]{1,0:T(8,128)} %idx_ref.11, f32[16,3328]{1,0:T(8,128)} %table_ref.3), custom_call_target="tpu_custom_call" | custom-call | tf_op jit(solution)/shard_map/up_product/pallas_call | solution.py:91
  121.9 1.3 dynamic-slice_bitcast_fusion
  123.8 2.0 collective-permute-done
  125.9 2.9 collective-permute-start.1
  128.9 1.4 convolution_bitcast_fusion
  130.3 8.7 %collective-permute-done.1 = f32[1,32,3328]{2,1,0:T(8,128)S(1)} collective-permute-done((f32[1,32,3328]{2,1,0:T(8,128)S(1)}, f32[1,32,3328]{2,1,0:T(8,128)S(1)}, u32[]{:S(2)}, u32[]{:S(2)}) %collective-permute-start.1) | collective-permute-done | bytes 426016 | tf_op jit(solution)/shard_map/ppermute | solution.py:277
  139.0 1.2 fusion.7
  140.3 1.8 collective-permute-start.2
  142.1 9.5 %collective-permute-done.2 = bf16[1,32,6656]{2,1,0:T(8,128)(2,1)S(1)} collective-permute-done((bf16[1,32,6656]{2,1,0:T(8,128)(2,1)S(1)}, bf16[1,32,6656]{2,1,0:T(8,128)(2,1)S(1)}, u32[]{:S(2)}, u32[]{:S(2)}) %collective-permute-start.2) | collective-permute-done | bytes 426016 | tf_op jit(solution)/shard_map/ppermute | solution.py:277
  151.9 2.4 collective-permute-done.3
  154.7 1.3 fusion.24
  156.0 36.6 %input_product.1 = f32[16,128,256]{2,1,0:T(8,128)} custom-call(bf16[128,3328]{1,0:T(8,128)(2,1)} %get-tuple-element.23.gate_ref.right_ref, bf16[128,3328]{1,0:T(8,128)(2,1)} %get-tuple-element.25.up_ref.right_ref, bf16[4096,3328]{1,0:T(8,128)(2,1)} %get-tuple-element.19.wg_ref, bf16[4096,3328]{1,0:T(8,128)(2,1)} %get-tuple-element.20.wu_ref), custom_call_target="tpu_custom_call" | custom-call | tf_op jit(solution)/shard_map/input_product/pallas_call | solution.py:172
  192.6 1.5 collective-permute-start.4
  194.2 5.8 %collective-permute-done.4 = bf16[1,32,3328]{2,1,0:T(8,128)(2,1)S(1)} collective-permute-done((bf16[1,32,3328]{2,1,0:T(8,128)(2,1)S(1)}, bf16[1,32,3328]{2,1,0:T(8,128)(2,1)S(1)}, u32[]{:S(2)}, u32[]{:S(2)}) %collective-permute-start.4) | collective-permute-done | bytes 213024 | tf_op jit(solution)/shard_map/ppermute | solution.py:277
  200.2 1.8 collective-permute-done.5
  202.8 1.4 fusion.left_ref
  204.1 63.3 %bins.3 = f32[16,4096]{1,0:T(8,128)} custom-call(bf16[13,256,128]{2,1,0:T(8,128)(2,1)} %fusion.left_ref, bf16[128,4096]{1,0:T(8,128)(2,1)} %right_ref.1, s32[1664,4096]{1,0:T(8,128)} %idx_ref.9), custom_call_target="tpu_custom_call" | custom-call | tf_op jit(solution)/shard_map/bins/pallas_call | solution.py:235
  267.5 64.1 %bins.4 = f32[16,3328]{1,0:T(8,128)} custom-call(bf16[16,256,128]{2,1,0:T(8,128)(2,1)} %bitcast.85, bf16[128,3328]{1,0:T(8,128)(2,1)} %get-tuple-element.23.gate_ref.right_ref, s32[2048,3328]{1,0:T(8,128)} %idx_ref.10), custom_call_target="tpu_custom_call" | custom-call | tf_op jit(solution)/shard_map/bins/pallas_call | solution.py:235
  331.5 8.4 %all-reduce.2.cloned.1.call-done = f32[16,4096]{1,0:T(8,128)} async-done(((f32[16,4096]{1,0:T(8,128)}), f32[16,4096]{1,0:T(8,128)}) %all-reduce.2.cloned.1.call-update) | async-done | bytes 262160 | tf_op jit(solution)/shard_map/psum | solution.py:357
  339.9 64.0 %bins.5 = f32[16,3328]{1,0:T(8,128)} custom-call(bf16[16,256,128]{2,1,0:T(8,128)(2,1)} %bitcast.86, bf16[128,3328]{1,0:T(8,128)(2,1)} %get-tuple-element.25.up_ref.right_ref, s32[2048,3328]{1,0:T(8,128)} %idx_ref.11), custom_call_target="tpu_custom_call" | custom-call | tf_op jit(solution)/shard_map/bins/pallas_call | solution.py:235
  403.9 1.0 pad_maximum_fusion.2
  405.0 1.8 collective-permute-done.6
  406.8 1.0 fusion.23
  407.8 1.5 collective-permute-start.7
  409.7 0.7 copy.36
  410.4 9.4 %collective-permute-done.7 = f32[16,6656]{1,0:T(8,128)S(1)} collective-permute-done((f32[16,6656]{1,0:T(8,128)S(1)}, f32[16,6656]{1,0:T(8,128)S(1)}, u32[]{:S(2)}, u32[]{:S(2)}) %collective-permute-start.7) | collective-permute-done | bytes 426016 | tf_op jit(solution)/shard_map/ppermute | solution.py:277
  419.8 0.8 fusion.25
  420.6 0.7 copy.42
  (45 shorter events, 3.6 us)
Async XLA Ops:
  7.2 121.7 %reduce-scatter.4.cloned.1.call-start = ((), (), s32[]{:S(2)}) async-start(), calls=%async_computation.3 | async-start | bytes 2129920 | tf_op jit(solution)/shard_map/reduce_scatter | solution.py:342
  47.9 1.2 copy-start.3
  48.0 91.0 %reduce-scatter.6.cloned.1.call-start = ((), (), s32[]{:S(2)}) async-start(), calls=%async_computation.4 | async-start | bytes 2129920 | tf_op jit(solution)/shard_map/reduce_scatter | solution.py:345
  49.7 36.7 %copy-start = (bf16[256,128,16]{1,0,2:T(8,128)(2,1)}, bf16[256,128,16]{1,0,2:T(8,128)(2,1)S(1)}, u32[]{:S(2)}) copy-start(bf16[256,128,16]{1,0,2:T(8,128)(2,1)S(1)} %convolution_convert_fusion) | copy-start | bytes 3145732
  86.4 181.0 %reduce-scatter.8.cloned.1.call-start = ((), (), s32[]{:S(2)}) async-start(), calls=%async_computation.5 | async-start | bytes 2359296 | tf_op jit(solution)/shard_map/reduce_scatter | solution.py:353
  121.9 3.9 copy-start.2
  123.2 2.6 collective-permute-start
  125.9 13.1 %collective-permute-start.1 = (f32[1,32,3328]{2,1,0:T(8,128)S(1)}, f32[1,32,3328]{2,1,0:T(8,128)S(1)}, u32[]{:S(2)}, u32[]{:S(2)}) collective-permute-start(f32[1,32,3328]{2,1,0:T(8,128)S(1)} %constant_dynamic-slice_fusion), channel_id=1, source_target_pairs={{0,16},{8,24},{16,0},{24,8},{1,17},{9,25},{17,1},{25,9},{2,18},{10... | collective-permute-start | bytes 1277960 | tf_op jit(solution)/shard_map/ppermute | solution.py:277
  140.3 11.3 %collective-permute-start.2 = (bf16[1,32,6656]{2,1,0:T(8,128)(2,1)S(1)}, bf16[1,32,6656]{2,1,0:T(8,128)(2,1)S(1)}, u32[]{:S(2)}, u32[]{:S(2)}) collective-permute-start(bf16[1,32,6656]{2,1,0:T(8,128)(2,1)S(1)} %maximum_bitcast_fusion.1), channel_id=1, source_target_pairs={{0,16},{8,24},{16,0},{24,8},{1,17},{9,25},{17,1},{25,9},{2,18},{10... | collective-permute-start | bytes 1277960 | tf_op jit(solution)/shard_map/ppermute | solution.py:277
  151.8 2.4 collective-permute-start.3
  192.6 147.3 %all-reduce.2.cloned.1.call-start = ((), (), s32[]{:S(2)}) async-start(), calls=%async_computation.6 | async-start | bytes 524288 | tf_op jit(solution)/shard_map/psum | solution.py:357
  192.6 7.4 %collective-permute-start.4 = (bf16[1,32,3328]{2,1,0:T(8,128)(2,1)S(1)}, bf16[1,32,3328]{2,1,0:T(8,128)(2,1)S(1)}, u32[]{:S(2)}, u32[]{:S(2)}) collective-permute-start(bf16[1,32,3328]{2,1,0:T(8,128)(2,1)S(1)} %bitcast.94), channel_id=1, source_target_pairs={{0,16},{8,24},{16,0},{24,8},{1,17},{9,25},{17,1},{25,9},{2,18},{10... | collective-permute-start | bytes 638984 | tf_op jit(solution)/shard_map/ppermute | solution.py:277
  200.1 1.8 collective-permute-start.5
  331.5 72.4 %copy-start.1 = (f32[16,3328]{1,0:T(8,128)S(1)}, f32[16,3328]{1,0:T(8,128)}, u32[]{:S(2)}) copy-start(f32[16,3328]{1,0:T(8,128)} %bins.4) | copy-start | bytes 638980
  403.9 5.4 %copy-start.4 = (f32[16,16,256]{2,1,0:T(8,128)S(1)}, f32[16,16,256]{2,1,0:T(8,128)}, u32[]{:S(2)}) copy-start(f32[16,16,256]{2,1,0:T(8,128)} %reduce-scatter.8.cloned.1.call-done) | copy-start | bytes 786436
  405.0 1.8 collective-permute-start.6
  407.8 12.8 %copy-start.5 = (f32[16,4096]{1,0:T(8,128)S(1)}, f32[16,4096]{1,0:T(8,128)}, u32[]{:S(2)}) copy-start(f32[16,4096]{1,0:T(8,128)} %all-reduce.2.cloned.1.call-done) | copy-start | bytes 786436
  407.8 11.9 %collective-permute-start.7 = (f32[16,6656]{1,0:T(8,128)S(1)}, f32[16,6656]{1,0:T(8,128)S(1)}, u32[]{:S(2)}, u32[]{:S(2)}) collective-permute-start(f32[16,6656]{1,0:T(8,128)S(1)} %fusion.23), channel_id=1, source_target_pairs={{0,16},{8,24},{16,0},{24,8},{1,17},{9,25},{17,1},{25,9},{2,18},{10... | collective-permute-start | bytes 1277960 | tf_op jit(solution)/shard_map/ppermute | solution.py:277
Sparse Core Ops, SparseCore 0:
  48.1 31.4 reduce-scatter.3
  86.5 31.5 reduce-scatter.5
  192.7 69.8 reduce-scatter.7
  267.6 72.2 all-reduce.1
